TPU v7x, 512 devices: a whole 4x8x8 slice. The times are simulated.
512 devices in a mesh: ep: 64 (over y, x, core), tp: 8 (over z).
Axes of the slice: x: 4, y: 8, z: 8, core: 2. Of those that a mesh axis runs over, the one named last changes fastest.
Arguments:
- attn: bfloat16 [512, 4096], P('ep', 'tp'), may hold values from -6 to 6
- resid: bfloat16 [512, 4096], P('ep'), may hold values from -3 to 3
- wo: bfloat16 [4096, 4096], P('tp', 'ep'), may hold values from -0.09375 to 0.09375
- norm_gain: float32 [4096], replicated, may hold values from 0.25 to 1.75
- router: bfloat16 [4096, 8], replicated, may hold values from -0.09375 to 0.09375
- expert_ids: int32 [512, 2], P('ep'), may hold values from 0 to 7, all different within a row; in each aligned block of 8 rows (0 to 7, 8 to 15, ...) at most 4 rows name the same one
- w_gate: bfloat16 [4096, 65536], P(None, ('ep', 'tp')), may hold values from -0.09375 to 0.09375
- w_up: bfloat16 [4096, 65536], P(None, ('ep', 'tp')), may hold values from -0.09375 to 0.09375
- w_down: bfloat16 [65536, 4096], P(('ep', 'tp')), may hold values from -0.1875 to 0.1875
- lengths: int32 [64, 4], P('ep'), may hold values from 1 to 4, 8 in all within a row
- final_gain: float32 [4096], replicated, may hold values from 0.25 to 1.75
- head: bfloat16 [16384, 4096], P(('ep', 'tp')), may hold values from -0.375 to 0.375
Outputs:
- mixed: bfloat16 [512, 4096], P('ep')
- max_logit: float32 [256], replicated
Inputs may be any that keep to these rules, and one draw needn't show every extreme that they name: `expert_ids`: the two ids of a row differ; among the 8 rows of one index of ep no expert is named by more than 4 rows, a bound that some block reaches. Each row of lengths sums to 8, and its largest entry is 4.
All inputs are finite; a program needn't handle non-finite values.
Results may differ from a plain program's by a relative error of at most 0.0075.
Values may be sent and summed in bfloat16 or wider, within the bound.
A program may use at most 192 MiB of HBM per device.

v0:
```python
import jax
import jax.numpy as jnp
from jax import lax
from jax.sharding import PartitionSpec as P


def rms_scale(values, gain):
    return values * lax.rsqrt(jnp.mean(values * values, axis=1, keepdims=True) + 1e-05) * gain


def local(
    attn, resid, wo, norm_gain, router, expert_ids, w_gate, w_up, w_down, lengths, final_gain, head
):
    row_count = resid.shape[0]
    width = resid.shape[1]
    ep_count = lax.axis_size("ep")
    expert_count = router.shape[1]
    group_size = ep_count // expert_count
    capacity = row_count // 2
    partial_proj = jnp.dot(
        attn, lax.all_gather(wo, "ep", axis=1, tiled=True), preferred_element_type=jnp.float32
    )
    proj = lax.psum(partial_proj, "tp")
    stream = resid.astype(jnp.float32) + proj
    normed = rms_scale(stream, norm_gain).astype(jnp.bfloat16)
    logits = jnp.dot(normed, router, preferred_element_type=jnp.float32)
    expert_range = jnp.arange(expert_count, dtype=jnp.int32)
    one_hot = (expert_ids[:, :, None] == expert_range).astype(jnp.float32)
    picked = jnp.sum(one_hot * logits[:, None, :], axis=2)
    first = 1.0 / (1.0 + jnp.exp(picked[:, 1] - picked[:, 0]))
    second = 1.0 / (1.0 + jnp.exp(picked[:, 0] - picked[:, 1]))
    both_weights = jnp.stack([first, second], axis=1)
    flat_hot = (expert_ids.reshape(-1)[:, None] == expert_range).astype(jnp.int32)
    earlier = jnp.cumsum(flat_hot, axis=0) - flat_hot
    slot_index = jnp.sum(earlier * flat_hot, axis=1)
    target = (expert_ids.reshape(-1) * capacity + slot_index).reshape(row_count, 2)
    slot_range = jnp.arange(expert_count * capacity, dtype=jnp.int32)
    placed = (target[:, :, None] == slot_range).astype(jnp.float32)
    dispatch_matrix = jnp.sum(placed, axis=1).astype(jnp.bfloat16)
    combine_matrix = jnp.sum(placed * both_weights[:, :, None], axis=1)
    send_rows = lax.dot_general(
        dispatch_matrix, normed, (((0,), (0,)), ((), ())), preferred_element_type=jnp.float32
    ).astype(jnp.bfloat16)
    per_expert = send_rows.reshape(expert_count, 1, capacity, width)
    outgoing = jnp.broadcast_to(per_expert, (expert_count, group_size, capacity, width))
    outgoing = outgoing.reshape(ep_count, capacity, width)
    arrived = lax.all_to_all(outgoing, "ep", split_axis=0, concat_axis=0, tiled=True)
    flat_rows = arrived.reshape(-1, width)
    gate = jnp.dot(flat_rows, w_gate, preferred_element_type=jnp.float32)
    upper = jnp.dot(flat_rows, w_up, preferred_element_type=jnp.float32)
    hidden = (jax.nn.silu(gate) * upper).astype(jnp.bfloat16)
    term = jnp.dot(hidden, w_down, preferred_element_type=jnp.float32).astype(jnp.bfloat16)
    term = term.reshape(arrived.shape[0], arrived.shape[1], width)
    returned = lax.all_to_all(term, "ep", split_axis=0, concat_axis=0, tiled=True)
    back_width = returned.shape[2]
    grouped = returned.reshape(expert_count, group_size, capacity, back_width).astype(jnp.float32)
    grouped = jnp.sum(grouped, axis=1).reshape(expert_count * capacity, back_width)
    expert_part = jnp.dot(
        combine_matrix, grouped, precision=lax.Precision.HIGHEST, preferred_element_type=jnp.float32
    )
    expert_total = lax.psum(expert_part, "tp")
    mixed = (stream + expert_total).astype(jnp.bfloat16)
    ends = jnp.cumsum(lengths[0]) - 1
    row_range = jnp.arange(row_count, dtype=jnp.int32)
    selector = (ends[:, None] == row_range).astype(jnp.bfloat16)
    last = jnp.dot(selector, mixed, preferred_element_type=jnp.float32)
    final = rms_scale(last, final_gain).astype(jnp.bfloat16)
    vocab_logits = lax.dot_general(
        lax.all_gather(final, "ep", axis=0, tiled=True),
        head,
        (((1,), (1,)), ((), ())),
        preferred_element_type=jnp.float32,
    )
    local_max = jnp.max(vocab_logits, axis=1)
    max_logit = lax.pmax(local_max, ("ep", "tp"))
    return (mixed, max_logit)


def solution(mesh):
    placed = (
        P("ep", "tp"),
        P("ep", None),
        P("tp", "ep"),
        P(),
        P(),
        P("ep", None),
        P(None, ("ep", "tp")),
        P(None, ("ep", "tp")),
        P(("ep", "tp"), None),
        P("ep", None),
        P(),
        P(("ep", "tp"), None),
    )
    return jax.shard_map(
        local, mesh=mesh, in_specs=placed, out_specs=(P("ep", None), P()), check_vma=False
    )
```

profile of v0, /device:TPU:1, one launch (start us, length us, event | category | flops | bytes accessed | tf_op | source)
XLA Modules:
  0.0 583.7 jit_solution(15072324507917972072)
XLA Ops:
  7.2 0.0 copy-start
  7.2 0.0 all-gather.4.cloned.1.call-start
  7.2 0.7 all-gather.4.cloned.1.call-update
  7.9 0.0 all-reduce.3.cloned.1.call-start
  8.0 0.8 copy.24
  8.7 0.1 eq.26
  8.8 0.1 fusion.8
  8.9 0.2 select_reduce_fusion.2
  9.1 0.1 reduce_sum.66
  9.2 0.0 copy-start.2
  9.2 0.0 copy-start.6
  9.2 0.0 copy-start.5
  9.2 0.0 copy-start.8
  9.2 92.4 %all-gather.4.cloned.1.call-done = bf16[512,4096]{0,1:T(8,128)(2,1)} async-done(((bf16[512,64]{0,1:T(8,128)(2,1)}), bf16[512,4096]{0,1:T(8,128)(2,1)}) %all-gather.4.cloned.1.call-update) | async-done | bytes 4194320 | tf_op jit(solution)/shard_map/all_gather | solution.py:21
  101.6 4.0 fusion.13
  105.6 0.0 all-reduce.3.cloned.1.call-update
  105.6 0.1 copy.26
  105.7 71.1 %all-reduce.3.cloned.1.call-done = f32[8,4096]{1,0:T(8,128)} async-done(((f32[8,4096]{1,0:T(8,128)}), f32[8,4096]{1,0:T(8,128)}) %all-reduce.3.cloned.1.call-update) | async-done | bytes 131088 | tf_op jit(solution)/shard_map/psum | solution.py:23
  176.8 0.0 copy-done.2
  176.8 1.1 multiply_reduce_fusion
  177.9 0.0 copy-done.6
  177.9 1.0 multiply_convert_fusion
  178.9 0.0 copy-done.5
  178.9 0.1 fusion.14
  179.0 0.0 copy-done.8
  179.0 0.2 select_reduce_fusion.1
  179.2 0.1 convert_reduce_fusion.1
  179.3 0.3 convolution_convert_fusion.1
  179.6 0.1 broadcast_in_dim.4
  179.7 1.0 broadcast_in_dim.5
  180.7 64.7 %all_to_all.10 = bf16[64,4,4096]{2,1,0:T(4,128)(2,1)} all-to-all(bf16[64,4,4096]{2,1,0:T(4,128)(2,1)S(1)} %bitcast.25), channel_id=1, replica_groups=mesh['ep'=64,'tp'=8] {'ep'}, dimensions={0} | all-to-all | bytes 4194304 | tf_op jit(solution)/shard_map/all_to_all | solution.py:47
  245.4 2.5 reshape.76
  248.0 1.9 fusion.15
  249.9 0.0 copy-done
  249.9 3.9 convolution_convert_fusion
  253.8 4.1 reshape.77
  257.9 0.0 copy-start.9
  257.9 7.1 %all-to-all-start.1 = ((bf16[64,4,4096]{2,1,0:T(4,128)(2,1)}), bf16[64,4,4096]{2,1,0:T(4,128)(2,1)S(1)}, u32[]{:S(2)}, u32[]{:S(2)}) async-start(bf16[64,4,4096]{2,1,0:T(4,128)(2,1)} %reshape.77), calls=%async_computation.1 | async-start | bytes 4194304 | tf_op jit(solution)/shard_map/all_to_all | solution.py:54
  265.0 0.0 all-reduce.5.cloned.1.call-start
  265.1 0.0 copy-done.9
  265.1 0.2 reduce-window.8
  265.3 0.0 copy-start.1
  265.3 0.0 copy-start.7
  265.3 49.5 %all-to-all-done.1 = bf16[64,4,4096]{2,1,0:T(4,128)(2,1)S(1)} async-done(((bf16[64,4,4096]{2,1,0:T(4,128)(2,1)}), bf16[64,4,4096]{2,1,0:T(4,128)(2,1)S(1)}, u32[]{:S(2)}, u32[]{:S(2)}) %all-to-all-start.1) | async-done | bytes 2097184 | tf_op jit(solution)/shard_map/all_to_all | solution.py:54
  314.7 1.9 convert_reduce_fusion
  316.6 1.2 reshape.78
  317.8 1.0 fusion.16
  318.9 0.0 all-reduce.5.cloned.1.call-update
  318.9 0.0 all-gather.6.cloned.1.call-start
  318.9 68.8 %all-reduce.5.cloned.1.call-done = f32[8,4096]{1,0:T(8,128)} async-done(((f32[8,4096]{1,0:T(8,128)}), f32[8,4096]{1,0:T(8,128)}) %all-reduce.5.cloned.1.call-update) | async-done | bytes 131088 | tf_op jit(solution)/shard_map/psum | solution.py:61
  387.7 0.0 copy-done.1
  387.7 0.9 add_convert_fusion
  388.6 0.0 copy-start.4
  388.7 0.3 multiply_reduce_fusion.1
  389.0 0.0 copy-done.7
  389.0 0.7 fusion.7
  389.7 0.0 all-gather.6.cloned.1.call-update
  389.7 0.0 copy-start.3
  389.7 87.1 %all-gather.6.cloned.1.call-done = bf16[64,4,4096]{2,1,0:T(4,128)(2,1)} async-done(((bf16[1,4,4096]{2,1,0:T(4,128)(2,1)}), bf16[64,4,4096]{2,1,0:T(4,128)(2,1)}) %all-gather.6.cloned.1.call-update) | async-done | bytes 2097168 | tf_op jit(solution)/shard_map/all_gather | solution.py:69
  476.8 2.5 reshape.82
  479.4 0.0 copy-done.4
  479.4 0.0 copy-done.3
  479.4 0.8 convolution_reduce_fusion
  480.1 97.0 %pmax.7 = f32[256]{0:T(256)} all-reduce(f32[256]{0:T(256)S(1)} %convolution_reduce_fusion), channel_id=1, replica_groups=mesh['ep'=64,'tp'=8] {'ep','tp'}, use_global_device_ids=true, to_apply=%region_12.13 | all-reduce | flops 256 | bytes 2048 | tf_op jit(solution)/shard_map/pmax | solution.py:75
  (7 shorter events, 0.1 us)
Async XLA Ops:
  7.2 242.7 %copy-start = (bf16[128,4096]{1,0:T(8,128)(2,1)S(1)}, bf16[128,4096]{1,0:T(8,128)(2,1)}, u32[]{:S(2)}) copy-start(bf16[128,4096]{1,0:T(8,128)(2,1)} %param.20) | copy-start | bytes 3145732
  7.2 94.4 %all-gather.4.cloned.1.call-start = ((), (), s32[]{:S(2)}) async-start(), calls=%async_computation.2 | async-start | bytes 4259840 | tf_op jit(solution)/shard_map/all_gather | solution.py:21
  7.9 168.9 %all-reduce.3.cloned.1.call-start = ((), (), s32[]{:S(2)}) async-start(), calls=%async_computation.3 | async-start | bytes 262144 | tf_op jit(solution)/shard_map/psum | solution.py:23
  9.2 167.6 %copy-start.2 = (bf16[8,4096]{1,0:T(8,128)(2,1)S(1)}, bf16[8,4096]{1,0:T(8,128)(2,1)}, u32[]{:S(2)}) copy-start(bf16[8,4096]{1,0:T(8,128)(2,1)} %param.13) | copy-start | bytes 196612
  9.2 168.7 %copy-start.6 = (f32[4096]{0:T(1024)S(1)}, f32[4096]{0:T(1024)}, u32[]{:S(2)}) copy-start(f32[4096]{0:T(1024)} %param.15) | copy-start | bytes 49156
  9.2 169.7 %copy-start.5 = (bf16[4096,8]{0,1:T(8,128)(2,1)S(1)}, bf16[4096,8]{0,1:T(8,128)(2,1)}, u32[]{:S(2)}) copy-start(bf16[4096,8]{0,1:T(8,128)(2,1)} %param.16) | copy-start | bytes 196612
  9.2 169.8 %copy-start.8 = (s32[8,2]{0,1:T(2,128)S(1)}, s32[8,2]{0,1:T(2,128)}, u32[]{:S(2)}) copy-start(s32[8,2]{0,1:T(2,128)} %param.17) | copy-start | bytes 196
  257.9 7.2 %copy-start.9 = (s32[1,4]{1,0:T(1,128)S(1)}, s32[1,4]{1,0:T(1,128)}, u32[]{:S(2)}) copy-start(s32[1,4]{1,0:T(1,128)} %param.21) | copy-start | bytes 52
  257.9 56.8 %all-to-all-start.1 = ((bf16[64,4,4096]{2,1,0:T(4,128)(2,1)}), bf16[64,4,4096]{2,1,0:T(4,128)(2,1)S(1)}, u32[]{:S(2)}, u32[]{:S(2)}) async-start(bf16[64,4,4096]{2,1,0:T(4,128)(2,1)} %reshape.77), calls=%async_computation.1 | async-start | bytes 4194304 | tf_op jit(solution)/shard_map/all_to_all | solution.py:54
  265.0 122.7 %all-reduce.5.cloned.1.call-start = ((), (), s32[]{:S(2)}) async-start(), calls=%async_computation.4 | async-start | bytes 262144 | tf_op jit(solution)/shard_map/psum | solution.py:61
  265.3 122.4 %copy-start.1 = (f32[8,4096]{1,0:T(8,128)S(1)}, f32[8,4096]{1,0:T(8,128)}, u32[]{:S(2)}) copy-start(f32[8,4096]{1,0:T(8,128)} %all-reduce.3.cloned.1.call-done) | copy-start | bytes 393220
  265.3 123.7 %copy-start.7 = (f32[4096]{0:T(1024)S(1)}, f32[4096]{0:T(1024)}, u32[]{:S(2)}) copy-start(f32[4096]{0:T(1024)} %param.22) | copy-start | bytes 49156
  318.9 157.9 %all-gather.6.cloned.1.call-start = ((), (), s32[]{:S(2)}) async-start(), calls=%async_computation.5 | async-start | bytes 2129920 | tf_op jit(solution)/shard_map/all_gather | solution.py:69
  388.6 90.7 %copy-start.4 = (bf16[8,4096]{1,0:T(8,128)(2,1)}, bf16[8,4096]{1,0:T(8,128)(2,1)S(1)}, u32[]{:S(2)}) copy-start(bf16[8,4096]{1,0:T(8,128)(2,1)S(1)} %add_convert_fusion) | copy-start | bytes 196612
  389.7 89.6 %copy-start.3 = (bf16[32,4096]{1,0:T(8,128)(2,1)S(1)}, bf16[32,4096]{1,0:T(8,128)(2,1)}, u32[]{:S(2)}) copy-start(bf16[32,4096]{1,0:T(8,128)(2,1)} %param.23) | copy-start | bytes 786436
Sparse Core Ops, SparseCore 0:
  11.3 90.1 all-gather.3
  105.7 71.0 all-reduce.2
  319.0 68.6 all-reduce.4
  390.9 85.8 all-gather.5
where the time goes:
time: 584 us
  waiting for transfers between devices  369 us (63%)
  blocking collectives  162 us (28%)
  between operations  14 us (2%)
  local copies, waits for them, and re-layouts  12.6 us (2%)
  matrix products  12.4 us (2%)
  starting transfers between devices  7.25 us (1%)
  other arithmetic  6.28 us (1%)
    pmax x1, blocking collectives, local(): max_logit = lax.pmax(local_max, ('ep', 'tp'))  97 us
    all_gather x1, waiting for transfers between devices, local(): lax.all_gather(wo, 'ep', axis=1, tiled=True)  92.4 us
    all_gather x1, waiting for transfers between devices, local(): lax.all_gather(final, 'ep', axis=0, tiled=True)  87.1 us
    psum x1, waiting for transfers between devices, local(): proj = lax.psum(partial_proj, 'tp')  71.1 us
    psum x1, waiting for transfers between devices, local(): expert_total = lax.psum(expert_part, 'tp')  68.8 us
    all_to_all x1, blocking collectives, local(): lax.all_to_all(outgoing, 'ep', split_axis=0, concat_axis=0, tiled=True)  64.7 us
    all_to_all x1, waiting for transfers between devices, local(): lax.all_to_all(term, 'ep', split_axis=0, concat_axis=0, tiled=True)  49.5 us
  transfers between devices with their start and end apart: 5, of which 5 were waited for; matrix products, arithmetic and copies ran while one was open for 0% of the time, Pallas kernels for 0%

commit v1 on v0

v1 whole, which is shorter than its diff:
```python
import jax
import jax.numpy as jnp
from jax import lax
from jax.experimental import pallas as pl
from jax.experimental.pallas import tpu as pltpu
from jax.sharding import PartitionSpec as P

F32 = jnp.float32
BF16 = jnp.bfloat16
NX, NY, NZ, NQ = 4, 8, 8, 32
MESH = pl.DeviceIdType.MESH
LOW = -3.0e38


def iota(shape, axis):
    return lax.broadcasted_iota(jnp.int32, shape, axis)


def mm(a, b):
    return jnp.dot(a, b, preferred_element_type=F32)


def near(i, t):
    half = (i + 1) // 2
    return (t + half * (2 * (i % 2) - 1) + NZ) % NZ


def kernel(
    attn, resid, wo, gain, router, ids, w_gate, w_up, w_down, lengths, final_gain, head,
    mixed, best,
    wo2, wg2, wu2, wd2, hd,
    at, p3, pb, pr, sb, xb, x32, eb, rb,
    db, yd, g, acc, tb, xr, zb, zr, yb, yr, mx, fr, lpb, rl, mq, mz,
    send, recv, gz, gx, tx, bg_send, bg_recv, bg_local,
):
    ep = lax.axis_index("ep")
    t = lax.axis_index("tp")
    q = ep // 2
    c = ep % 2
    y = q // NX
    x = q % NX

    def at_q(k):
        return (2 * k + c, t)

    def at_z(k):
        return (ep, k)

    def at_y(k):
        return ((k * NX + x) * 2 + c, t)

    def at_x(k):
        return ((y * NX + k) * 2 + c, t)

    def at_cz(k):
        return (2 * q + k // NZ, k % NZ)

    other = (2 * q + 1 - c, t)
    mine_cz = c * NZ + t

    def each(count, me, body):
        def step(d, carry):
            body((me + d) % count)
            return carry

        lax.fori_loop(1, count, step, 0)

    def push(src, dst, where, send_sem, recv_sem):
        pltpu.make_async_remote_copy(
            src_ref=src, dst_ref=dst, send_sem=send_sem, recv_sem=recv_sem,
            device_id=where, device_id_type=MESH,
        ).start()

    def drain(ref, sem):
        pltpu.make_async_copy(ref, ref, sem).wait()

    barrier = pltpu.get_barrier_semaphore()

    def hello(where):
        pl.semaphore_signal(barrier, inc=1, device_id=where, device_id_type=MESH)

    each(NQ, q, lambda k: hello(at_q(k)))
    each(2 * NZ, mine_cz, lambda k: hello(at_cz(k)))
    at[q] = attn[...]
    pl.semaphore_wait(barrier, NQ - 1 + 2 * NZ - 1)

    each(NQ, q, lambda k: push(at.at[q], at.at[q], at_q(k), send.at[0], recv.at[0]))

    pairs = ((wo, wo2), (w_gate, wg2), (w_up, wu2), (w_down, wd2))
    for n, (src, dst) in enumerate(pairs):
        push(src, dst.at[c], other, bg_send.at[n], bg_recv.at[n])
        pltpu.make_async_copy(src, dst.at[c], bg_local.at[n]).start()

    def head_part(k):
        return head.at[:, pl.ds(pl.multiple_of((k % NZ) * 512, 512), 512)]

    each(2 * NZ, mine_cz, lambda k: push(
        head_part(k), hd.at[mine_cz], at_cz(k), bg_send.at[4], bg_recv.at[4]))
    pltpu.make_async_copy(head_part(t), hd.at[mine_cz], bg_local.at[4]).start()

    rows = resid[...].astype(F32)
    row = jnp.sum(jnp.where(iota(rows.shape, 0) == t, rows, 0.0), axis=0, keepdims=True)
    for k in range(NQ):
        x32[k:k + 1, :] = row[:, 128 * k:128 * k + 128]

    id0 = ids[:, 0:1]
    id1 = ids[:, 1:2]
    id0_32 = jnp.concatenate([id0] * 4, axis=0)
    id1_32 = jnp.concatenate([id1] * 4, axis=0)
    r_i = iota((32, 128), 0)
    c_i = iota((32, 128), 1)
    col_k = c_i >> 4
    is0 = id0_32 == col_k
    is1 = id1_32 == col_k
    member = jnp.where(is0 | is1, 1.0, 0.0)
    lr = iota((32, 32), 0)
    lc = iota((32, 32), 1)
    lower = jnp.where(((lr >> 3) == (lc >> 3)) & (lc < lr), 1.0, 0.0)
    earlier = mm(lower.astype(BF16), member.astype(BF16))
    slot = (c_i & 3).astype(F32)
    placed = jnp.where(
        (jnp.abs(earlier - slot) < 0.5) & ((r_i >> 3) == ((c_i >> 2) & 3)), member, 0.0)
    ra = iota((128, 128), 0)
    ca = iota((128, 128), 1)
    perm = jnp.where(ca == 16 * ((ra >> 2) & 7) + 4 * (ra >> 5) + (ra & 3), 1.0, 0.0).astype(BF16)
    perm_t = jnp.where(ra == 16 * ((ca >> 2) & 7) + 4 * (ca >> 5) + (ca & 3), 1.0, 0.0).astype(BF16)

    for n in range(1):
        drain(wo2.at[1 - c], bg_recv.at[n])
        drain(wo2.at[c], bg_local.at[n])
    drain(at.at[pl.ds(0, NQ - 1)], recv.at[0])
    a = at[...].astype(F32).reshape(256, 512).astype(BF16)
    part = jnp.concatenate([mm(a, wo2[0]), mm(a, wo2[1])], axis=1)
    p3[...] = part.reshape(NQ, 8, 128)
    for r in range(NZ):
        pb[r] = p3[:, r, :]
    each(NZ, t, lambda k: push(pb.at[k], pr.at[t], at_z(k), send.at[1], recv.at[1]))
    pr[t] = pb[t]
    drain(pr.at[pl.ds(0, NZ - 1)], recv.at[1])
    sb[:, 0, :] = jnp.sum(pr[...], axis=0)
    each(NQ, q, lambda k: push(sb.at[k], xb.at[q], at_q(k), send.at[2], recv.at[2]))
    xb[q] = sb[q]
    drain(xb.at[pl.ds(0, NQ - 1)], recv.at[2])

    xrow = x32[...] + xb[:, 0, :]
    x32[...] = xrow
    scale = lax.rsqrt(jnp.sum(xrow * xrow, keepdims=True) * (1.0 / 4096) + 1e-05)
    hrow = (xrow * scale * gain[...]).astype(BF16).astype(F32)
    lane = iota((1, 128), 1)
    stats = jnp.where(lane == 0, scale, 0.0)
    for k in range(8):
        one = jnp.sum(hrow * router[k].astype(F32), keepdims=True)
        stats = stats + jnp.where(lane == 8 + k, one, 0.0)
    eb[...] = jnp.zeros_like(eb)
    for k in range(NZ):
        eb[k, 0:4, :] = x32[4 * k:4 * k + 4, :]
        eb[k, 4:5, :] = stats
    each(NZ, t, lambda k: push(eb.at[k], rb.at[t], at_z(k), send.at[3], recv.at[3]))
    rb[t] = eb[t]
    drain(rb.at[pl.ds(0, NZ - 1)], recv.at[3])

    xs = jnp.concatenate([rb[:, j, :] for j in range(4)], axis=0)
    st = rb[:, 4, :]
    scale32 = jnp.concatenate([st[:, 0:1]] * 4, axis=0)
    gain32 = jnp.concatenate(
        [jnp.broadcast_to(gain[pl.ds(4 * t + j, 1), :], (8, 128)) for j in range(4)], axis=0)
    fgain32 = jnp.concatenate(
        [jnp.broadcast_to(final_gain[pl.ds(4 * t + j, 1), :], (8, 128)) for j in range(4)], axis=0)
    h32 = (xs * scale32 * gain32).astype(BF16)
    lane8 = iota((8, 128), 1)
    la = jnp.sum(jnp.where(lane8 == id0 + 8, st, 0.0), axis=1, keepdims=True)
    lb = jnp.sum(jnp.where(lane8 == id1 + 8, st, 0.0), axis=1, keepdims=True)
    wa = 1.0 / (1.0 + jnp.exp(lb - la))
    wb = 1.0 / (1.0 + jnp.exp(la - lb))
    wa32 = jnp.concatenate([wa] * 4, axis=0)
    wb32 = jnp.concatenate([wb] * 4, axis=0)
    combine = placed * jnp.where(is0, wa32, wb32)

    disp = lax.dot_general(
        placed.astype(BF16), h32, (((0,), (0,)), ((), ())), preferred_element_type=F32)
    db[...] = disp.astype(BF16).reshape(NY, 16, 128)
    each(NY, y, lambda k: push(db.at[k], yd.at[y], at_y(k), send.at[4], recv.at[4]))
    yd[y] = db[y]
    drain(yd.at[pl.ds(0, NY - 1)], recv.at[4])
    slots = mm(perm, yd[...].reshape(128, 128)).astype(BF16)
    for j in range(4):
        g[x, t, :, 128 * j:128 * j + 128] = slots[32 * j:32 * j + 32, :]
    each(NZ, t, lambda k: push(g.at[x, t], g.at[x, t], at_z(k), send.at[5], gz.at[t]))
    each(NX, x, lambda k: push(g.at[x, t], g.at[x, t], at_x(k), send.at[6], gx.at[t]))

    def forward(i, carry):
        z = near(i, t)
        drain(g.at[x, z], gz.at[z])
        each(NX, x, lambda k: push(g.at[x, z], g.at[x, z], at_x(k), send.at[6], gx.at[z]))
        return carry

    lax.fori_loop(1, NZ, forward, 0)

    for n in (1, 2, 3):
        dst = pairs[n][1]
        drain(dst.at[1 - c], bg_recv.at[n])
        drain(dst.at[c], bg_local.at[n])
    acc[...] = jnp.zeros_like(acc)

    def up_step(i, carry):
        z = near(i, t)
        drain(g.at[pl.ds(0, NX - 1), z], gx.at[z])
        lhs = g[:, z].reshape(128, 512)
        start = pl.multiple_of(z * 512, 512)
        for k in range(2):
            acc[k] += mm(lhs, wg2[k, pl.ds(start, 512), :])
            acc[2 + k] += mm(lhs, wu2[k, pl.ds(start, 512), :])
        return carry

    lax.fori_loop(0, NZ, up_step, 0)
    hidden = jnp.concatenate(
        [acc[k] * jax.nn.sigmoid(acc[k]) * acc[2 + k] for k in range(2)], axis=1).astype(BF16)

    def down_step(i, carry):
        z = near(NZ - 1 - i, t)
        start = pl.multiple_of(z * 512, 512)
        term = mm(hidden, wd2[:, :, pl.ds(start, 512)].reshape(256, 512))
        tb[:, z] = term.reshape(NX, 32, 512).astype(BF16)
        each(NX, x, lambda k: push(tb.at[k, z], xr.at[x, z], at_x(k), send.at[7], tx.at[z]))
        xr[x, z] = tb[x, z]
        return carry

    lax.fori_loop(0, NZ, down_step, 0)

    def sum_x(z):
        drain(xr.at[pl.ds(0, NX - 1), z], tx.at[z])
        return jnp.sum(xr[:, z].astype(F32), axis=0).astype(BF16)

    def sum_step(i, carry):
        z = near(NZ - 1 - i, t)
        zb[z] = sum_x(z)
        push(zb.at[z], zr.at[t], at_z(z), send.at[8], recv.at[8])
        return carry

    lax.fori_loop(0, NZ - 1, sum_step, 0)
    zr[t] = sum_x(t)
    drain(zr.at[pl.ds(0, NZ - 1)], recv.at[8])
    total = jnp.sum(zr[...].astype(F32), axis=0)
    stacked = jnp.concatenate(
        [total[:, 128 * j:128 * j + 128] for j in range(4)], axis=0).astype(BF16)
    yb[...] = mm(perm_t, stacked).astype(BF16).reshape(NY, 16, 128)
    each(NY, y, lambda k: push(yb.at[k], yr.at[y], at_y(k), send.at[9], recv.at[9]))
    yr[y] = yb[y]
    drain(yr.at[pl.ds(0, NY - 1)], recv.at[9])

    back = yr[...].reshape(128, 128).astype(F32)
    out32 = jnp.dot(combine, back, precision=lax.Precision.HIGHEST, preferred_element_type=F32)
    mx[t] = (xs + out32).astype(BF16)
    each(NZ, t, lambda k: push(mx.at[t], mx.at[t], at_z(k), send.at[10], recv.at[10]))
    drain(mx.at[pl.ds(0, NZ - 1)], recv.at[10])
    m3 = mx[...].astype(F32)
    mixed[...] = jnp.concatenate(
        [m3[z, 8 * j:8 * j + 8, :] for z in range(NZ) for j in range(4)], axis=1).astype(BF16)

    ss = jnp.sum(jnp.sum(m3 * m3, axis=0), axis=1, keepdims=True)
    ss8 = ss[0:8] + ss[8:16] + ss[16:24] + ss[24:32]
    scale2 = lax.rsqrt(ss8 * (1.0 / 4096) + 1e-05)
    own = mx[t].astype(F32)
    fin = (own * jnp.concatenate([scale2] * 4, axis=0) * fgain32).astype(BF16)
    lens = jnp.broadcast_to(lengths[...], (16, 4))
    ends = jnp.sum(
        jnp.where(iota((16, 4), 1) <= (iota((16, 4), 0) & 3), lens, 0), axis=1, keepdims=True) - 1
    sr = iota((16, 32), 0)
    sc = iota((16, 32), 1)
    pick = jnp.where(((sr >> 2) == (sc >> 3)) & (ends == (sc & 7)), 1.0, 0.0).astype(BF16)
    fr[q] = mm(pick, fin).astype(BF16)
    each(NQ, q, lambda k: push(fr.at[q], fr.at[q], at_q(k), send.at[11], recv.at[11]))
    drain(hd.at[pl.ds(0, 2 * NZ - 1)], bg_recv.at[4])
    drain(hd.at[0], bg_local.at[4])
    drain(fr.at[pl.ds(0, NQ - 1)], recv.at[11])

    rows512 = fr[...].reshape(512, 128)
    vocab = hd[...].reshape(512, 512)
    fa = iota((128, 512), 0)
    fb = iota((128, 512), 1)
    logits = jnp.zeros((128, 512), F32)
    for j in range(4):
        order = jnp.where(fb == 16 * (fa >> 2) + 4 * j + (fa & 3), 1.0, 0.0).astype(BF16)
        rows_j = mm(order, rows512).astype(BF16)
        logits = logits + lax.dot_general(
            rows_j, vocab[:, 128 * j:128 * j + 128], (((1,), (1,)), ((), ())),
            preferred_element_type=F32)
    lpb[...] = logits.reshape(NZ, 16, 512)
    each(NZ, t, lambda k: push(lpb.at[k], rl.at[t], at_z(k), send.at[12], recv.at[12]))
    rl[t] = lpb[t]
    drain(rl.at[pl.ds(0, NZ - 1)], recv.at[12])
    top = jnp.max(jnp.sum(rl[...], axis=0), axis=1, keepdims=True)
    spread = jnp.where(iota((16, 128), 1) == iota((16, 128), 0) + 16 * t, top, LOW)
    mq[q] = jnp.max(spread, axis=0, keepdims=True)
    each(NQ, q, lambda k: push(mq.at[q], mq.at[q], at_q(k), send.at[13], recv.at[13]))
    drain(mq.at[pl.ds(0, NQ - 1)], recv.at[13])
    mz[mine_cz] = jnp.max(mq[:, 0, :], axis=0, keepdims=True)
    each(2 * NZ, mine_cz, lambda k: push(
        mz.at[mine_cz], mz.at[mine_cz], at_cz(k), send.at[14], recv.at[14]))
    drain(mz.at[pl.ds(0, 2 * NZ - 1)], recv.at[14])
    both = mz[:, 0, :]
    best[0:1, :] = jnp.max(both[0:8], axis=0, keepdims=True)
    best[1:2, :] = jnp.max(both[8:16], axis=0, keepdims=True)

    for n, (src, dst) in enumerate(pairs):
        drain(dst.at[c], bg_send.at[n])
    drain(hd.at[pl.ds(0, 2 * NZ - 1)], bg_send.at[4])
    sent = (
        at.at[pl.ds(0, NQ - 1)], pb.at[pl.ds(0, NZ - 1)], sb.at[pl.ds(0, NQ - 1)],
        eb.at[pl.ds(0, NZ - 1)], db.at[pl.ds(0, NY - 1)], g.at[0, pl.ds(0, NZ - 1)],
        g.at[pl.ds(0, NX - 1)], tb.at[pl.ds(0, NX - 1)], zb.at[pl.ds(0, NZ - 1)],
        yb.at[pl.ds(0, NY - 1)], mx.at[pl.ds(0, NZ - 1)], fr.at[pl.ds(0, NQ - 1)],
        lpb.at[pl.ds(0, NZ - 1)], mq.at[pl.ds(0, NQ - 1)], mz.at[pl.ds(0, 2 * NZ - 1)],
    )
    for n, ref in enumerate(sent):
        drain(ref, send.at[n])


def local(
    attn, resid, wo, norm_gain, router, expert_ids, w_gate, w_up, w_down, lengths, final_gain, head
):
    vm = pl.BlockSpec(memory_space=pltpu.VMEM)
    hbm = pl.BlockSpec(memory_space=pl.ANY)
    v = pltpu.VMEM
    dma = pltpu.SemaphoreType.DMA
    mixed, best = pl.pallas_call(
        kernel,
        out_shape=(
            jax.ShapeDtypeStruct((8, 4096), BF16),
            jax.ShapeDtypeStruct((2, 128), F32),
        ),
        in_specs=[vm, vm, hbm, vm, vm, vm, hbm, hbm, hbm, vm, vm, hbm],
        out_specs=(vm, vm),
        scratch_shapes=[
            v((2, 512, 64), BF16), v((2, 4096, 128), BF16), v((2, 4096, 128), BF16),
            v((2, 128, 4096), BF16), v((16, 32, 512), BF16),
            v((NQ, 8, 512), BF16), v((NQ, 8, 128), F32), v((NZ, NQ, 128), F32),
            v((NZ, NQ, 128), F32), v((NQ, 1, 128), F32), v((NQ, 1, 128), F32),
            v((NQ, 128), F32), v((NZ, 8, 128), F32), v((NZ, 8, 128), F32),
            v((NY, 16, 128), BF16), v((NY, 16, 128), BF16), v((NX, NZ, 32, 512), BF16),
            v((4, 128, 128), F32), v((NX, NZ, 32, 512), BF16), v((NX, NZ, 32, 512), BF16),
            v((NZ, 32, 512), BF16), v((NZ, 32, 512), BF16), v((NY, 16, 128), BF16),
            v((NY, 16, 128), BF16), v((NZ, 32, 128), BF16), v((NQ, 16, 128), BF16),
            v((NZ, 16, 512), F32), v((NZ, 16, 512), F32), v((NQ, 1, 128), F32),
            v((2 * NZ, 1, 128), F32),
            dma((15,)), dma((15,)), dma((NZ,)), dma((NZ,)), dma((NZ,)),
            dma((5,)), dma((5,)), dma((5,)),
        ],
        compiler_params=pltpu.CompilerParams(
            collective_id=0, has_side_effects=True, vmem_limit_bytes=48 << 20),
    )(
        attn, resid, wo, norm_gain.reshape(NQ, 128), router.T.reshape(8, NQ, 128), expert_ids,
        w_gate, w_up, w_down, lengths, final_gain.reshape(NQ, 128), head,
    )
    max_logit = best.reshape(2, NQ, 4).transpose(1, 0, 2).reshape(256)
    return mixed, max_logit


def solution(mesh):
    placed = (
        P("ep", "tp"),
        P("ep", None),
        P("tp", "ep"),
        P(),
        P(),
        P("ep", None),
        P(None, ("ep", "tp")),
        P(None, ("ep", "tp")),
        P(("ep", "tp"), None),
        P("ep", None),
        P(),
        P(("ep", "tp"), None),
    )
    return jax.shard_map(
        local, mesh=mesh, in_specs=placed, out_specs=(P("ep", None), P()), check_vma=False
    )
```

time: 584 us -> 125 us (0.21)
  waiting for transfers between devices: 369 us -> 0 us
  blocking collectives: 162 us -> 0 us
  Pallas kernels: 0 us -> 114 us
  between operations: 14 us -> 0.74 us
  matrix products: 12.4 us -> 0 us
  starting transfers between devices: 7.25 us -> 0 us
  other arithmetic: 6.28 us -> 0 us
    all_gather x2 -> x0, waiting for transfers between devices: 179 us -> none  [the longest x1 92.4 us: local(): lax.all_gather(wo, 'ep', axis=1, tiled=True)]
    psum x2 -> x0, waiting for transfers between devices: 140 us -> none  [the longest x1 71.1 us: local(): proj = lax.psum(partial_proj, 'tp')]
    pallas_call x0 -> x1, Pallas kernels: none -> 114 us  [local(): pl.pallas_call(kernel, out_shape=(jax.ShapeDtypeStruct((8, 4096), BF16),...]
    pmax x1 -> x0, blocking collectives: 97 us -> none  [local(): max_logit = lax.pmax(local_max, ('ep', 'tp'))]
    all_to_all x1 -> x0, blocking collectives: 64.7 us -> none  [local(): lax.all_to_all(outgoing, 'ep', split_axis=0, concat_axis=0, tiled=True)]
    all_to_all x1 -> x0, waiting for transfers between devices: 49.5 us -> none  [local(): lax.all_to_all(term, 'ep', split_axis=0, concat_axis=0, tiled=True)]
    dot_general x8 -> x0, matrix products: 12.4 us -> none  [the longest x1 4.03 us: local(): jnp.dot(attn, lax.all_gather(wo, 'ep', axis=1, tiled=True), preferred_ele...]
    reshape x3 -> x2, local copies, waits for them, and re-layouts: 7.88 us -> 0.78 us  [local(): max_logit = best.reshape(2, NQ, 4).transpose(1, 0, 2).reshape(256)]
  transfers between devices with their start and end apart: 5 -> 0, of which waited for: 5 -> 0; matrix products, arithmetic and copies ran while one was open for 0% -> 0% of each run, Pallas kernels for 0% -> 0%
where the time goes in v1:
time: 125 us; the launch traced here: 124 us
  Pallas kernels  114 us (91%)
  local copies, waits for them, and re-layouts  9.19 us (7%)
    pallas_call x1, Pallas kernels, local(): pl.pallas_call(kernel, out_shape=(jax.ShapeDtypeStruct((8, 4096), BF16),...  114 us
    unnamed x22, local copies, waits for them, and re-layouts  8.38 us

profile of v1, /device:TPU:1, one launch (start us, length us, event | category | flops | bytes accessed | tf_op | source)
XLA Modules:
  0.0 124.3 jit_solution(6406854897797792952)
XLA Ops:
  0.6 0.0 copy-start.3
  0.6 0.8 copy.17.ids
  1.4 0.8 copy.21
  2.3 0.0 copy-start.4
  2.3 0.0 copy-start.7
  2.3 0.0 copy-start.8
  2.3 1.0 copy.16.wo
  3.3 0.0 copy-done.3
  3.3 0.0 copy-done.4
  3.3 0.0 copy-done.7
  3.3 0.0 copy-done.8
  3.4 0.0 copy-start
  3.4 1.2 copy-done
  4.6 0.0 copy-start.1
  4.6 1.2 copy-done.1
  5.8 0.0 copy-start.2
  5.8 1.2 copy-done.2
  7.0 0.0 copy-start.5
  7.0 0.7 copy-done.5
  7.8 0.0 copy-start.6
  7.8 0.7 copy-done.6
  8.5 114.3 %shard_map.131 = (bf16[8,4096]{1,0:T(8,128)(2,1)S(1)}, f32[2,128]{1,0:T(2,128)S(1)}) custom-call(bf16[8,512]{1,0:T(8,128)(2,1)S(1)} %copy-done.7, bf16[8,4096]{1,0:T(8,128)(2,1)S(1)} %copy-done.4, bf16[512,64]{1,0:T(8,128)(2,1)S(1)} %copy.16.wo, f32[32,128]{1,0:T(8,128)S(1)} %bitcast.9, bf16[8,32,128]{2,1,0:T(8,128)(2,1)S(1)} %bitcast.8, ...), custom_call_target="tpu_custom_call" | custom-call | tf_op jit(solution)/shard_map/pallas_call | solution.py:326
  122.8 0.1 reshape.22
  123.0 0.7 reshape.23
  123.6 0.6 copy.23
  (1 shorter events, 0.0 us)
Async XLA Ops:
  0.6 2.7 %copy-start.3 = (bf16[32,4096]{1,0:T(8,128)(2,1)S(1)}, bf16[32,4096]{1,0:T(8,128)(2,1)}, u32[]{:S(2)}) copy-start(bf16[32,4096]{1,0:T(8,128)(2,1)} %head.1) | copy-start | bytes 786436
  2.3 1.0 copy-start.4
  2.3 1.0 copy-start.7
  2.3 1.0 copy-start.8
  3.4 1.2 copy-start
  4.6 1.2 copy-start.1
  5.8 1.2 copy-start.2
  7.0 0.7 copy-start.5
  7.8 0.7 copy-start.6

commit v2 on v1

--- a/solution.py
+++ b/solution.py
@@ -26,12 +26,13 @@
 
 
 def kernel(
-    attn, resid, wo, gain, router, ids, w_gate, w_up, w_down, lengths, final_gain, head,
+    attn, resid_in, wo, gain_in, router_in, ids_in, w_gate, w_up, w_down, lengths_in, fgain_in,
+    head,
     mixed, best,
-    wo2, wg2, wu2, wd2, hd,
+    resid, gain, router, ids, lengths, final_gain, wo2, wg2, wu2, wd2, hd,
     at, p3, pb, pr, sb, xb, x32, eb, rb,
-    db, yd, g, acc, tb, xr, zb, zr, yb, yr, mx, fr, lpb, rl, mq, mz,
-    send, recv, gz, gx, tx, bg_send, bg_recv, bg_local,
+    db, yd, g, acc, tb, xr, zb, zr, yb, yr, mx, fr, lpb, rl, mq, mz, order,
+    send, recv, gz, gx, tx, bg_send, bg_recv, bg_local, small,
 ):
     ep = lax.axis_index("ep")
     t = lax.axis_index("tp")
@@ -74,6 +75,13 @@
     def drain(ref, sem):
         pltpu.make_async_copy(ref, ref, sem).wait()
 
+    inputs = (
+        (attn, at.at[q]), (resid_in, resid), (gain_in, gain), (router_in, router),
+        (ids_in, ids), (lengths_in, lengths), (fgain_in, final_gain),
+    )
+    for n, (src, dst) in enumerate(inputs):
+        pltpu.make_async_copy(src, dst, small.at[n]).start()
+
     barrier = pltpu.get_barrier_semaphore()
 
     def hello(where):
@@ -81,30 +89,34 @@
 
     each(NQ, q, lambda k: hello(at_q(k)))
     each(2 * NZ, mine_cz, lambda k: hello(at_cz(k)))
-    at[q] = attn[...]
+    drain(at.at[q], small.at[0])
     pl.semaphore_wait(barrier, NQ - 1 + 2 * NZ - 1)
 
     each(NQ, q, lambda k: push(at.at[q], at.at[q], at_q(k), send.at[0], recv.at[0]))
 
     pairs = ((wo, wo2), (w_gate, wg2), (w_up, wu2), (w_down, wd2))
-    for n, (src, dst) in enumerate(pairs):
+
+    def swap(n):
+        src, dst = pairs[n]
         push(src, dst.at[c], other, bg_send.at[n], bg_recv.at[n])
         pltpu.make_async_copy(src, dst.at[c], bg_local.at[n]).start()
 
+    swap(0)
+
     def head_part(k):
         return head.at[:, pl.ds(pl.multiple_of((k % NZ) * 512, 512), 512)]
 
-    each(2 * NZ, mine_cz, lambda k: push(
-        head_part(k), hd.at[mine_cz], at_cz(k), bg_send.at[4], bg_recv.at[4]))
-    pltpu.make_async_copy(head_part(t), hd.at[mine_cz], bg_local.at[4]).start()
+    for n in range(1, len(inputs)):
+        drain(inputs[n][1], small.at[n])
 
     rows = resid[...].astype(F32)
     row = jnp.sum(jnp.where(iota(rows.shape, 0) == t, rows, 0.0), axis=0, keepdims=True)
     for k in range(NQ):
         x32[k:k + 1, :] = row[:, 128 * k:128 * k + 128]
 
-    id0 = ids[:, 0:1]
-    id1 = ids[:, 1:2]
+    eye = iota((8, 8), 0) == iota((8, 8), 1)
+    id0 = jnp.sum(jnp.where(eye, ids[0:1, :], 0), axis=1, keepdims=True)
+    id1 = jnp.sum(jnp.where(eye, ids[1:2, :], 0), axis=1, keepdims=True)
     id0_32 = jnp.concatenate([id0] * 4, axis=0)
     id1_32 = jnp.concatenate([id1] * 4, axis=0)
     r_i = iota((32, 128), 0)
@@ -125,12 +137,25 @@
     perm = jnp.where(ca == 16 * ((ra >> 2) & 7) + 4 * (ra >> 5) + (ra & 3), 1.0, 0.0).astype(BF16)
     perm_t = jnp.where(ra == 16 * ((ca >> 2) & 7) + 4 * (ca >> 5) + (ca & 3), 1.0, 0.0).astype(BF16)
 
-    for n in range(1):
-        drain(wo2.at[1 - c], bg_recv.at[n])
-        drain(wo2.at[c], bg_local.at[n])
+    lens = jnp.broadcast_to(lengths[...], (16, 4))
+    ends = jnp.sum(
+        jnp.where(iota((16, 4), 1) <= (iota((16, 4), 0) & 3), lens, 0), axis=1, keepdims=True) - 1
+    sr = iota((16, 32), 0)
+    sc = iota((16, 32), 1)
+    pick = jnp.where(((sr >> 2) == (sc >> 3)) & (ends == (sc & 7)), 1.0, 0.0).astype(BF16)
+    fa = iota((128, 512), 0)
+    fb = iota((128, 512), 1) - 16 * (fa >> 2) - (fa & 3)
+    for j in range(4):
+        order[j] = jnp.where(fb == 4 * j, 1.0, 0.0).astype(BF16)
+
+    drain(wo2.at[1 - c], bg_recv.at[0])
+    drain(wo2.at[c], bg_local.at[0])
     drain(at.at[pl.ds(0, NQ - 1)], recv.at[0])
+    for n in (1, 2, 3):
+        swap(n)
     a = at[...].astype(F32).reshape(256, 512).astype(BF16)
-    part = jnp.concatenate([mm(a, wo2[0]), mm(a, wo2[1])], axis=1)
+    part = lax.dot_general(
+        a, wo2[...].reshape(128, 512), (((1,), (1,)), ((), ())), preferred_element_type=F32)
     p3[...] = part.reshape(NQ, 8, 128)
     for r in range(NZ):
         pb[r] = p3[:, r, :]
@@ -143,14 +168,17 @@
     drain(xb.at[pl.ds(0, NQ - 1)], recv.at[2])
 
     xrow = x32[...] + xb[:, 0, :]
-    x32[...] = xrow
     scale = lax.rsqrt(jnp.sum(xrow * xrow, keepdims=True) * (1.0 / 4096) + 1e-05)
     hrow = (xrow * scale * gain[...]).astype(BF16).astype(F32)
     lane = iota((1, 128), 1)
-    stats = jnp.where(lane == 0, scale, 0.0)
-    for k in range(8):
-        one = jnp.sum(hrow * router[k].astype(F32), keepdims=True)
-        stats = stats + jnp.where(lane == 8 + k, one, 0.0)
+    x32[...] = hrow
+    dots = jnp.zeros((8, 128), F32)
+    for k in range(NQ):
+        dots = dots + x32[k:k + 1, :] * router[:, 128 * k:128 * k + 128].astype(F32)
+    x32[...] = xrow
+    dots = jnp.sum(dots, axis=1, keepdims=True)
+    put = jnp.where(iota((8, 128), 1) == iota((8, 128), 0) + 8, dots, 0.0)
+    stats = jnp.where(lane == 0, scale, 0.0) + jnp.sum(put, axis=0, keepdims=True)
     eb[...] = jnp.zeros_like(eb)
     for k in range(NZ):
         eb[k, 0:4, :] = x32[4 * k:4 * k + 4, :]
@@ -164,8 +192,6 @@
     scale32 = jnp.concatenate([st[:, 0:1]] * 4, axis=0)
     gain32 = jnp.concatenate(
         [jnp.broadcast_to(gain[pl.ds(4 * t + j, 1), :], (8, 128)) for j in range(4)], axis=0)
-    fgain32 = jnp.concatenate(
-        [jnp.broadcast_to(final_gain[pl.ds(4 * t + j, 1), :], (8, 128)) for j in range(4)], axis=0)
     h32 = (xs * scale32 * gain32).astype(BF16)
     lane8 = iota((8, 128), 1)
     la = jnp.sum(jnp.where(lane8 == id0 + 8, st, 0.0), axis=1, keepdims=True)
@@ -175,6 +201,10 @@
     wa32 = jnp.concatenate([wa] * 4, axis=0)
     wb32 = jnp.concatenate([wb] * 4, axis=0)
     combine = placed * jnp.where(is0, wa32, wb32)
+
+    each(NZ, t, lambda k: push(
+        head_part(k), hd.at[mine_cz], at_z(k), bg_send.at[4], bg_recv.at[4]))
+    pltpu.make_async_copy(head_part(t), hd.at[mine_cz], bg_local.at[4]).start()
 
     disp = lax.dot_general(
         placed.astype(BF16), h32, (((0,), (0,)), ((), ())), preferred_element_type=F32)
@@ -248,49 +278,48 @@
     yr[y] = yb[y]
     drain(yr.at[pl.ds(0, NY - 1)], recv.at[9])
 
+    mine = hd.at[pl.ds(c * NZ, NZ)]
+    drain(hd.at[pl.ds(0, NZ - 1)], bg_recv.at[4])
+    drain(hd.at[0], bg_local.at[4])
+    push(mine, mine, other, bg_send.at[5], bg_recv.at[5])
+
     back = yr[...].reshape(128, 128).astype(F32)
     out32 = jnp.dot(combine, back, precision=lax.Precision.HIGHEST, preferred_element_type=F32)
-    mx[t] = (xs + out32).astype(BF16)
+    own = (xs + out32).astype(BF16)
+    mx[t] = own
+    fr[q] = mm(pick, own).astype(BF16)
+    each(NQ, q, lambda k: push(fr.at[q], fr.at[q], at_q(k), send.at[11], recv.at[11]))
     each(NZ, t, lambda k: push(mx.at[t], mx.at[t], at_z(k), send.at[10], recv.at[10]))
+    drain(mine, bg_recv.at[5])
+    drain(fr.at[pl.ds(0, NQ - 1)], recv.at[11])
+
+    rows512 = fr[...].reshape(512, 128)
+    vocab = hd[...].reshape(512, 512)
+    logits = jnp.zeros((128, 512), F32)
+    squares = jnp.zeros((128, 128), F32)
+    for j in range(4):
+        rows_j = mm(order[j], rows512)
+        squares = squares + rows_j * rows_j
+        fin = (rows_j * final_gain[pl.ds(4 * t + j, 1), :]).astype(BF16)
+        logits = logits + lax.dot_general(
+            fin, vocab[:, 128 * j:128 * j + 128], (((1,), (1,)), ((), ())),
+            preferred_element_type=F32)
+    squares = jnp.broadcast_to(jnp.sum(squares, axis=1, keepdims=True), (128, 128))
+    lpb[:, :, 0:512] = logits.reshape(NZ, 16, 512)
+    lpb[:, :, 512:640] = squares.reshape(NZ, 16, 128)
+    each(NZ, t, lambda k: push(lpb.at[k], rl.at[t], at_z(k), send.at[12], recv.at[12]))
+    rl[t] = lpb[t]
     drain(mx.at[pl.ds(0, NZ - 1)], recv.at[10])
     m3 = mx[...].astype(F32)
     mixed[...] = jnp.concatenate(
         [m3[z, 8 * j:8 * j + 8, :] for z in range(NZ) for j in range(4)], axis=1).astype(BF16)
-
-    ss = jnp.sum(jnp.sum(m3 * m3, axis=0), axis=1, keepdims=True)
-    ss8 = ss[0:8] + ss[8:16] + ss[16:24] + ss[24:32]
-    scale2 = lax.rsqrt(ss8 * (1.0 / 4096) + 1e-05)
-    own = mx[t].astype(F32)
-    fin = (own * jnp.concatenate([scale2] * 4, axis=0) * fgain32).astype(BF16)
-    lens = jnp.broadcast_to(lengths[...], (16, 4))
-    ends = jnp.sum(
-        jnp.where(iota((16, 4), 1) <= (iota((16, 4), 0) & 3), lens, 0), axis=1, keepdims=True) - 1
-    sr = iota((16, 32), 0)
-    sc = iota((16, 32), 1)
-    pick = jnp.where(((sr >> 2) == (sc >> 3)) & (ends == (sc & 7)), 1.0, 0.0).astype(BF16)
-    fr[q] = mm(pick, fin).astype(BF16)
-    each(NQ, q, lambda k: push(fr.at[q], fr.at[q], at_q(k), send.at[11], recv.at[11]))
-    drain(hd.at[pl.ds(0, 2 * NZ - 1)], bg_recv.at[4])
-    drain(hd.at[0], bg_local.at[4])
-    drain(fr.at[pl.ds(0, NQ - 1)], recv.at[11])
-
-    rows512 = fr[...].reshape(512, 128)
-    vocab = hd[...].reshape(512, 512)
-    fa = iota((128, 512), 0)
-    fb = iota((128, 512), 1)
-    logits = jnp.zeros((128, 512), F32)
-    for j in range(4):
-        order = jnp.where(fb == 16 * (fa >> 2) + 4 * j + (fa & 3), 1.0, 0.0).astype(BF16)
-        rows_j = mm(order, rows512).astype(BF16)
-        logits = logits + lax.dot_general(
-            rows_j, vocab[:, 128 * j:128 * j + 128], (((1,), (1,)), ((), ())),
-            preferred_element_type=F32)
-    lpb[...] = logits.reshape(NZ, 16, 512)
-    each(NZ, t, lambda k: push(lpb.at[k], rl.at[t], at_z(k), send.at[12], recv.at[12]))
-    rl[t] = lpb[t]
     drain(rl.at[pl.ds(0, NZ - 1)], recv.at[12])
-    top = jnp.max(jnp.sum(rl[...], axis=0), axis=1, keepdims=True)
-    spread = jnp.where(iota((16, 128), 1) == iota((16, 128), 0) + 16 * t, top, LOW)
+    summed = jnp.sum(rl[...], axis=0)
+    scale2 = lax.rsqrt(summed[:, 512:513] * (1.0 / 4096) + 1e-05)
+    top = jnp.max(summed[:, 0:512], axis=1, keepdims=True) * scale2
+    vr = iota((16, 128), 0)
+    place = (4 * (t % 4) + (vr >> 2)) * 8 + 4 * c + (vr & 3)
+    spread = jnp.where(iota((16, 128), 1) == place, top, LOW)
     mq[q] = jnp.max(spread, axis=0, keepdims=True)
     each(NQ, q, lambda k: push(mq.at[q], mq.at[q], at_q(k), send.at[13], recv.at[13]))
     drain(mq.at[pl.ds(0, NQ - 1)], recv.at[13])
@@ -298,13 +327,16 @@
     each(2 * NZ, mine_cz, lambda k: push(
         mz.at[mine_cz], mz.at[mine_cz], at_cz(k), send.at[14], recv.at[14]))
     drain(mz.at[pl.ds(0, 2 * NZ - 1)], recv.at[14])
-    both = mz[:, 0, :]
-    best[0:1, :] = jnp.max(both[0:8], axis=0, keepdims=True)
-    best[1:2, :] = jnp.max(both[8:16], axis=0, keepdims=True)
+    for k in range(2):
+        both = [mz[m * NZ + 4 * k + n] for m in range(2) for n in range(4)]
+        while len(both) > 1:
+            both = [jnp.maximum(a, b) for a, b in zip(both[::2], both[1::2])]
+        best[k:k + 1, :] = both[0]
 
     for n, (src, dst) in enumerate(pairs):
         drain(dst.at[c], bg_send.at[n])
-    drain(hd.at[pl.ds(0, 2 * NZ - 1)], bg_send.at[4])
+    drain(hd.at[pl.ds(0, NZ - 1)], bg_send.at[4])
+    drain(hd.at[pl.ds(0, NZ)], bg_send.at[5])
     sent = (
         at.at[pl.ds(0, NQ - 1)], pb.at[pl.ds(0, NZ - 1)], sb.at[pl.ds(0, NQ - 1)],
         eb.at[pl.ds(0, NZ - 1)], db.at[pl.ds(0, NY - 1)], g.at[0, pl.ds(0, NZ - 1)],
@@ -329,10 +361,12 @@
             jax.ShapeDtypeStruct((8, 4096), BF16),
             jax.ShapeDtypeStruct((2, 128), F32),
         ),
-        in_specs=[vm, vm, hbm, vm, vm, vm, hbm, hbm, hbm, vm, vm, hbm],
+        in_specs=[hbm] * 12,
         out_specs=(vm, vm),
         scratch_shapes=[
-            v((2, 512, 64), BF16), v((2, 4096, 128), BF16), v((2, 4096, 128), BF16),
+            v((8, 4096), BF16), v((NQ, 128), F32), v((8, 4096), BF16), v((2, 8), jnp.int32),
+            v((1, 4), jnp.int32), v((NQ, 128), F32),
+            v((2, 64, 512), BF16), v((2, 4096, 128), BF16), v((2, 4096, 128), BF16),
             v((2, 128, 4096), BF16), v((16, 32, 512), BF16),
             v((NQ, 8, 512), BF16), v((NQ, 8, 128), F32), v((NZ, NQ, 128), F32),
             v((NZ, NQ, 128), F32), v((NQ, 1, 128), F32), v((NQ, 1, 128), F32),
@@ -341,19 +375,18 @@
             v((4, 128, 128), F32), v((NX, NZ, 32, 512), BF16), v((NX, NZ, 32, 512), BF16),
             v((NZ, 32, 512), BF16), v((NZ, 32, 512), BF16), v((NY, 16, 128), BF16),
             v((NY, 16, 128), BF16), v((NZ, 32, 128), BF16), v((NQ, 16, 128), BF16),
-            v((NZ, 16, 512), F32), v((NZ, 16, 512), F32), v((NQ, 1, 128), F32),
-            v((2 * NZ, 1, 128), F32),
+            v((NZ, 16, 640), F32), v((NZ, 16, 640), F32), v((NQ, 1, 128), F32),
+            v((2 * NZ, 1, 128), F32), v((4, 128, 512), BF16),
             dma((15,)), dma((15,)), dma((NZ,)), dma((NZ,)), dma((NZ,)),
-            dma((5,)), dma((5,)), dma((5,)),
+            dma((6,)), dma((6,)), dma((6,)), dma((7,)),
         ],
         compiler_params=pltpu.CompilerParams(
-            collective_id=0, has_side_effects=True, vmem_limit_bytes=48 << 20),
+            collective_id=0, has_side_effects=True, vmem_limit_bytes=63 << 20),
     )(
-        attn, resid, wo, norm_gain.reshape(NQ, 128), router.T.reshape(8, NQ, 128), expert_ids,
+        attn, resid, wo.T, norm_gain.reshape(NQ, 128), router.T, expert_ids.T,
         w_gate, w_up, w_down, lengths, final_gain.reshape(NQ, 128), head,
     )
-    max_logit = best.reshape(2, NQ, 4).transpose(1, 0, 2).reshape(256)
-    return mixed, max_logit
+    return mixed, best.reshape(256)
 
 
 def solution(mesh):

time: 125 us -> 113 us (0.904)
  local copies, waits for them, and re-layouts: 9.19 us -> 2.04 us
  Pallas kernels: 114 us -> 110 us
    unnamed x22 -> x4, local copies, waits for them, and re-layouts: 8.38 us -> 2.04 us
    pallas_call x1, Pallas kernels: 114 us -> 110 us  [local(): pl.pallas_call(kernel, out_shape=(jax.ShapeDtypeStruct((8, 4096), BF16),...]
where the time goes in v2:
time: 113 us
  Pallas kernels  110 us (97%)
  local copies, waits for them, and re-layouts  2.04 us (2%)
    pallas_call x1, Pallas kernels, local(): pl.pallas_call(kernel, out_shape=(jax.ShapeDtypeStruct((8, 4096), BF16),...  110 us

profile of v2, /device:TPU:1, one launch (start us, length us, event | category | flops | bytes accessed | tf_op | source)
XLA Modules:
  0.0 112.8 jit_solution(8031578639775857790)
XLA Ops:
  0.6 110.1 %shard_map.131 = (bf16[8,4096]{1,0:T(8,128)(2,1)}, f32[2,128]{1,0:T(2,128)}) custom-call(bf16[8,512]{1,0:T(8,128)(2,1)} %attn.1, bf16[8,4096]{1,0:T(8,128)(2,1)} %resid_in.1, bf16[64,512]{1,0:T(8,128)(2,1)} %bitcast.6, f32[32,128]{1,0:T(8,128)} %bitcast.8, bf16[8,4096]{1,0:T(8,128)(2,1)} %bitcast.7, s32[2,8]{1,0:T(2,128)} %bitcast.10, ...), custom_call_target="tpu_custom_call" | custom-call | tf_op jit(solution)/shard_map/pallas_call | solution.py:358
  110.8 0.0 copy-start
  110.8 1.5 %copy.16 = bf16[8,4096]{1,0:T(8,128)(2,1)} copy(bf16[8,4096]{1,0:T(8,128)(2,1)} %get-tuple-element.8) | data formatting | bytes 131072
  112.3 0.0 copy-done
  112.3 0.6 copy.17
Async XLA Ops:
  110.8 1.5 %copy-start = (f32[2,128]{1,0:T(2,128)S(1)}, f32[2,128]{1,0:T(2,128)}, u32[]{:S(2)}) copy-start(f32[2,128]{1,0:T(2,128)} %get-tuple-element.5) | copy-start | bytes 3076

commit v3 on v2

--- a/solution.py
+++ b/solution.py
@@ -32,7 +32,7 @@
     resid, gain, router, ids, lengths, final_gain, wo2, wg2, wu2, wd2, hd,
     at, p3, pb, pr, sb, xb, x32, eb, rb,
     db, yd, g, acc, tb, xr, zb, zr, yb, yr, mx, fr, lpb, rl, mq, mz, order,
-    send, recv, gz, gx, tx, bg_send, bg_recv, bg_local, small,
+    send, recv, gz, gx, tx, bg_send, bg_recv, bg_local, small, g_left, g_right,
 ):
     ep = lax.axis_index("ep")
     t = lax.axis_index("tp")
@@ -216,15 +216,36 @@
     for j in range(4):
         g[x, t, :, 128 * j:128 * j + 128] = slots[32 * j:32 * j + 32, :]
     each(NZ, t, lambda k: push(g.at[x, t], g.at[x, t], at_z(k), send.at[5], gz.at[t]))
-    each(NX, x, lambda k: push(g.at[x, t], g.at[x, t], at_x(k), send.at[6], gx.at[t]))
-
-    def forward(i, carry):
+    right = (x + 1) % NX
+    left = (x + NX - 1) % NX
+
+    def spread_x(z):
+        push(g.at[x, z], g.at[x, z], at_x(right), send.at[6], g_left.at[z])
+        push(g.at[x, z], g.at[x, z], at_x(left), send.at[6], g_right.at[z])
+
+    def pass_on(z):
+        drain(g.at[left, z], g_left.at[z])
+        part = g.at[left, z, pl.ds(0, 16)]
+        push(part, part, at_x(right), send.at[15], gx.at[z])
+        drain(g.at[right, z], g_right.at[z])
+        part = g.at[right, z, pl.ds(16, 16)]
+        push(part, part, at_x(left), send.at[15], gx.at[z])
+
+    def arrive(i):
         z = near(i, t)
         drain(g.at[x, z], gz.at[z])
-        each(NX, x, lambda k: push(g.at[x, z], g.at[x, z], at_x(k), send.at[6], gx.at[z]))
+        spread_x(z)
+
+    def forward(i, carry):
+        arrive(i)
+        pass_on(near(i - 2, t))
         return carry
 
-    lax.fori_loop(1, NZ, forward, 0)
+    spread_x(t)
+    arrive(1)
+    lax.fori_loop(2, NZ, forward, 0)
+    pass_on(near(NZ - 2, t))
+    pass_on(near(NZ - 1, t))
 
     for n in (1, 2, 3):
         dst = pairs[n][1]
@@ -234,7 +255,7 @@
 
     def up_step(i, carry):
         z = near(i, t)
-        drain(g.at[pl.ds(0, NX - 1), z], gx.at[z])
+        drain(g.at[0, z], gx.at[z])
         lhs = g[:, z].reshape(128, 512)
         start = pl.multiple_of(z * 512, 512)
         for k in range(2):
@@ -305,8 +326,8 @@
             fin, vocab[:, 128 * j:128 * j + 128], (((1,), (1,)), ((), ())),
             preferred_element_type=F32)
     squares = jnp.broadcast_to(jnp.sum(squares, axis=1, keepdims=True), (128, 128))
-    lpb[:, :, 0:512] = logits.reshape(NZ, 16, 512)
-    lpb[:, :, 512:640] = squares.reshape(NZ, 16, 128)
+    lpb[:, :, 0:512] = logits.reshape(NZ, 16, 512).astype(BF16)
+    lpb[:, :, 512:640] = squares.reshape(NZ, 16, 128).astype(BF16)
     each(NZ, t, lambda k: push(lpb.at[k], rl.at[t], at_z(k), send.at[12], recv.at[12]))
     rl[t] = lpb[t]
     drain(mx.at[pl.ds(0, NZ - 1)], recv.at[10])
@@ -314,7 +335,7 @@
     mixed[...] = jnp.concatenate(
         [m3[z, 8 * j:8 * j + 8, :] for z in range(NZ) for j in range(4)], axis=1).astype(BF16)
     drain(rl.at[pl.ds(0, NZ - 1)], recv.at[12])
-    summed = jnp.sum(rl[...], axis=0)
+    summed = jnp.sum(rl[...].astype(F32), axis=0)
     scale2 = lax.rsqrt(summed[:, 512:513] * (1.0 / 4096) + 1e-05)
     top = jnp.max(summed[:, 0:512], axis=1, keepdims=True) * scale2
     vr = iota((16, 128), 0)
@@ -340,9 +361,10 @@
     sent = (
         at.at[pl.ds(0, NQ - 1)], pb.at[pl.ds(0, NZ - 1)], sb.at[pl.ds(0, NQ - 1)],
         eb.at[pl.ds(0, NZ - 1)], db.at[pl.ds(0, NY - 1)], g.at[0, pl.ds(0, NZ - 1)],
-        g.at[pl.ds(0, NX - 1)], tb.at[pl.ds(0, NX - 1)], zb.at[pl.ds(0, NZ - 1)],
+        g.at[pl.ds(0, 2)], tb.at[pl.ds(0, NX - 1)], zb.at[pl.ds(0, NZ - 1)],
         yb.at[pl.ds(0, NY - 1)], mx.at[pl.ds(0, NZ - 1)], fr.at[pl.ds(0, NQ - 1)],
         lpb.at[pl.ds(0, NZ - 1)], mq.at[pl.ds(0, NQ - 1)], mz.at[pl.ds(0, 2 * NZ - 1)],
+        g.at[0],
     )
     for n, ref in enumerate(sent):
         drain(ref, send.at[n])
@@ -375,10 +397,10 @@
             v((4, 128, 128), F32), v((NX, NZ, 32, 512), BF16), v((NX, NZ, 32, 512), BF16),
             v((NZ, 32, 512), BF16), v((NZ, 32, 512), BF16), v((NY, 16, 128), BF16),
             v((NY, 16, 128), BF16), v((NZ, 32, 128), BF16), v((NQ, 16, 128), BF16),
-            v((NZ, 16, 640), F32), v((NZ, 16, 640), F32), v((NQ, 1, 128), F32),
+            v((NZ, 16, 640), BF16), v((NZ, 16, 640), BF16), v((NQ, 1, 128), F32),
             v((2 * NZ, 1, 128), F32), v((4, 128, 512), BF16),
-            dma((15,)), dma((15,)), dma((NZ,)), dma((NZ,)), dma((NZ,)),
-            dma((6,)), dma((6,)), dma((6,)), dma((7,)),
+            dma((16,)), dma((15,)), dma((NZ,)), dma((NZ,)), dma((NZ,)),
+            dma((6,)), dma((6,)), dma((6,)), dma((7,)), dma((NZ,)), dma((NZ,)),
         ],
         compiler_params=pltpu.CompilerParams(
             collective_id=0, has_side_effects=True, vmem_limit_bytes=63 << 20),

time: 113 us -> 115 us (1.018)
  Pallas kernels: 110 us -> 112 us
    pallas_call x1, Pallas kernels: 110 us -> 112 us  [local(): pl.pallas_call(kernel, out_shape=(jax.ShapeDtypeStruct((8, 4096), BF16),...]
where the time goes in v3:
time: 115 us
  Pallas kernels  112 us (97%)
  local copies, waits for them, and re-layouts  2.04 us (2%)
    pallas_call x1, Pallas kernels, local(): pl.pallas_call(kernel, out_shape=(jax.ShapeDtypeStruct((8, 4096), BF16),...  112 us

profile of v3, /device:TPU:1, one launch (start us, length us, event | category | flops | bytes accessed | tf_op | source)
XLA Modules:
  0.0 114.9 jit_solution(14339508158047102161)
XLA Ops:
  0.6 112.2 %shard_map.131 = (bf16[8,4096]{1,0:T(8,128)(2,1)}, f32[2,128]{1,0:T(2,128)}) custom-call(bf16[8,512]{1,0:T(8,128)(2,1)} %attn.1, bf16[8,4096]{1,0:T(8,128)(2,1)} %resid_in.1, bf16[64,512]{1,0:T(8,128)(2,1)} %bitcast.6, f32[32,128]{1,0:T(8,128)} %bitcast.8, bf16[8,4096]{1,0:T(8,128)(2,1)} %bitcast.7, s32[2,8]{1,0:T(2,128)} %bitcast.10, ...), custom_call_target="tpu_custom_call" | custom-call | tf_op jit(solution)/shard_map/pallas_call | solution.py:380
  112.9 0.0 copy-start
  112.9 1.5 %copy.16 = bf16[8,4096]{1,0:T(8,128)(2,1)} copy(bf16[8,4096]{1,0:T(8,128)(2,1)} %get-tuple-element.8) | data formatting | bytes 131072
  114.3 0.0 copy-done
  114.4 0.6 copy.17
Async XLA Ops:
  112.9 1.5 %copy-start = (f32[2,128]{1,0:T(2,128)S(1)}, f32[2,128]{1,0:T(2,128)}, u32[]{:S(2)}) copy-start(f32[2,128]{1,0:T(2,128)} %get-tuple-element.5) | copy-start | bytes 3076

commit v4 on v2

--- a/solution.py
+++ b/solution.py
@@ -105,6 +105,10 @@
 
     def head_part(k):
         return head.at[:, pl.ds(pl.multiple_of((k % NZ) * 512, 512), 512)]
+
+    each(NZ, t, lambda k: push(
+        head_part(k), hd.at[mine_cz], at_z(k), bg_send.at[4], bg_recv.at[4]))
+    pltpu.make_async_copy(head_part(t), hd.at[mine_cz], bg_local.at[4]).start()
 
     for n in range(1, len(inputs)):
         drain(inputs[n][1], small.at[n])
@@ -202,10 +206,6 @@
     wb32 = jnp.concatenate([wb] * 4, axis=0)
     combine = placed * jnp.where(is0, wa32, wb32)
 
-    each(NZ, t, lambda k: push(
-        head_part(k), hd.at[mine_cz], at_z(k), bg_send.at[4], bg_recv.at[4]))
-    pltpu.make_async_copy(head_part(t), hd.at[mine_cz], bg_local.at[4]).start()
-
     disp = lax.dot_general(
         placed.astype(BF16), h32, (((0,), (0,)), ((), ())), preferred_element_type=F32)
     db[...] = disp.astype(BF16).reshape(NY, 16, 128)
@@ -305,8 +305,8 @@
             fin, vocab[:, 128 * j:128 * j + 128], (((1,), (1,)), ((), ())),
             preferred_element_type=F32)
     squares = jnp.broadcast_to(jnp.sum(squares, axis=1, keepdims=True), (128, 128))
-    lpb[:, :, 0:512] = logits.reshape(NZ, 16, 512)
-    lpb[:, :, 512:640] = squares.reshape(NZ, 16, 128)
+    lpb[:, :, 0:512] = logits.reshape(NZ, 16, 512).astype(BF16)
+    lpb[:, :, 512:640] = squares.reshape(NZ, 16, 128).astype(BF16)
     each(NZ, t, lambda k: push(lpb.at[k], rl.at[t], at_z(k), send.at[12], recv.at[12]))
     rl[t] = lpb[t]
     drain(mx.at[pl.ds(0, NZ - 1)], recv.at[10])
@@ -314,7 +314,7 @@
     mixed[...] = jnp.concatenate(
         [m3[z, 8 * j:8 * j + 8, :] for z in range(NZ) for j in range(4)], axis=1).astype(BF16)
     drain(rl.at[pl.ds(0, NZ - 1)], recv.at[12])
-    summed = jnp.sum(rl[...], axis=0)
+    summed = jnp.sum(rl[...].astype(F32), axis=0)
     scale2 = lax.rsqrt(summed[:, 512:513] * (1.0 / 4096) + 1e-05)
     top = jnp.max(summed[:, 0:512], axis=1, keepdims=True) * scale2
     vr = iota((16, 128), 0)
@@ -375,7 +375,7 @@
             v((4, 128, 128), F32), v((NX, NZ, 32, 512), BF16), v((NX, NZ, 32, 512), BF16),
             v((NZ, 32, 512), BF16), v((NZ, 32, 512), BF16), v((NY, 16, 128), BF16),
             v((NY, 16, 128), BF16), v((NZ, 32, 128), BF16), v((NQ, 16, 128), BF16),
-            v((NZ, 16, 640), F32), v((NZ, 16, 640), F32), v((NQ, 1, 128), F32),
+            v((NZ, 16, 640), BF16), v((NZ, 16, 640), BF16), v((NQ, 1, 128), F32),
             v((2 * NZ, 1, 128), F32), v((4, 128, 512), BF16),
             dma((15,)), dma((15,)), dma((NZ,)), dma((NZ,)), dma((NZ,)),
             dma((6,)), dma((6,)), dma((6,)), dma((7,)),

time: 113 us -> 111 us (0.982)
  Pallas kernels: 110 us -> 108 us
    pallas_call x1, Pallas kernels: 110 us -> 108 us  [local(): pl.pallas_call(kernel, out_shape=(jax.ShapeDtypeStruct((8, 4096), BF16),...]
where the time goes in v4:
time: 111 us
  Pallas kernels  108 us (97%)
  local copies, waits for them, and re-layouts  2.04 us (2%)
    pallas_call x1, Pallas kernels, local(): pl.pallas_call(kernel, out_shape=(jax.ShapeDtypeStruct((8, 4096), BF16),...  108 us

profile of v4, /device:TPU:1, one launch (start us, length us, event | category | flops | bytes accessed | tf_op | source)
XLA Modules:
  0.0 111.0 jit_solution(17177482652283666100)
XLA Ops:
  0.6 108.3 %shard_map.131 = (bf16[8,4096]{1,0:T(8,128)(2,1)}, f32[2,128]{1,0:T(2,128)}) custom-call(bf16[8,512]{1,0:T(8,128)(2,1)} %attn.1, bf16[8,4096]{1,0:T(8,128)(2,1)} %resid_in.1, bf16[64,512]{1,0:T(8,128)(2,1)} %bitcast.6, f32[32,128]{1,0:T(8,128)} %bitcast.8, bf16[8,4096]{1,0:T(8,128)(2,1)} %bitcast.7, s32[2,8]{1,0:T(2,128)} %bitcast.10, ...), custom_call_target="tpu_custom_call" | custom-call | tf_op jit(solution)/shard_map/pallas_call | solution.py:358
  109.0 0.0 copy-start
  109.0 1.5 %copy.16 = bf16[8,4096]{1,0:T(8,128)(2,1)} copy(bf16[8,4096]{1,0:T(8,128)(2,1)} %get-tuple-element.8) | data formatting | bytes 131072
  110.4 0.0 copy-done
  110.4 0.6 copy.17
Async XLA Ops:
  109.0 1.5 %copy-start = (f32[2,128]{1,0:T(2,128)S(1)}, f32[2,128]{1,0:T(2,128)}, u32[]{:S(2)}) copy-start(f32[2,128]{1,0:T(2,128)} %get-tuple-element.5) | copy-start | bytes 3076
